TPU v7x, 32 devices: a whole 2x2x4 slice. The times are simulated.
32 devices in a mesh: tm: 8 (over z, x), space: 4 (over y, core).
Axes of the slice: x: 2, y: 2, z: 4, core: 2. Of those that a mesh axis runs over, the one named last changes fastest.
Arguments:
- queries: bfloat16 [8, 512, 2048], P('tm', 'space'), may hold values from -180 to 180
- key_vectors: bfloat16 [8, 512, 2048], P('tm', 'space'), may hold values from -6 to 6
- value_vectors: bfloat16 [8, 512, 2048], P('tm', 'space'), may hold values from -96 to 96
- block_lists: int32 [4, 3], replicated, may hold values from 0 to 3, as said below
- step_sizes: float32 [8, 512, 16], P(None, ('space', 'tm')), may hold values from 0.004 to 0.6, as said below
- decay_rates: float32 [16], replicated, may hold values from 0.7 to 1.4
- skip_gains: float32 [16], replicated, may hold values from 0.5 to 1.5
- pre_gain: float32 [2048], replicated, may hold values from 0.25 to 1.75
- state_in_weight: bfloat16 [2048, 64], replicated, may hold values from -0.125 to 0.125
- state_out_weight: bfloat16 [2048, 64], replicated, may hold values from -0.125 to 0.125
- post_gain: float32 [2048], replicated, may hold values from 0.25 to 1.75
Outputs:
- mixed_out: bfloat16 [8, 512, 2048], P('tm', 'space')
Inputs may be any that keep to these rules, and one draw needn't show every extreme that they name: `block_lists`: row i lists 3 different key blocks; its first entry is i itself. `step_sizes`: positive step sizes.
All inputs are finite; a program needn't handle non-finite values.
Results may differ from a plain program's by a relative error of at most 0.01.
Values may be sent and summed in bfloat16 or wider, within the bound.
A program may use at most 64 MiB of HBM per device.

v0:
```python
import math
import jax
import jax.numpy as jnp
from jax import lax
from jax.sharding import PartitionSpec as P

SHARED_HEADS = 16
HEAD_DIM = 128
BLOCK = 128


def rms_scale(values, gain_row):
    return values * lax.rsqrt(jnp.mean(values * values, axis=-1, keepdims=True) + 1e-05) * gain_row


def attend_heads(stacked, block_lists):
    query_rows, key_rows, value_rows = stacked
    total_rows, head_count, head_width = query_rows.shape
    block_count = total_rows // BLOCK
    group_size = math.gcd(block_count, max(1, 512 // BLOCK))
    list_width = block_lists.shape[1]
    score_scale = 1.0 / math.sqrt(head_width)
    query_blocks = query_rows.reshape(block_count, BLOCK, head_count, head_width)
    key_blocks = key_rows.reshape(block_count, BLOCK, head_count, head_width)
    value_blocks = value_rows.reshape(block_count, BLOCK, head_count, head_width)

    def attend_group(group_index):
        first_block = group_index * group_size
        chosen = lax.dynamic_slice_in_dim(block_lists, first_block, group_size, 0)
        query_group = lax.dynamic_slice_in_dim(query_blocks, first_block, group_size, 0)
        key_group = jnp.take(key_blocks, chosen, axis=0).reshape(
            group_size, list_width * BLOCK, head_count, head_width
        )
        value_group = jnp.take(value_blocks, chosen, axis=0).reshape(
            group_size, list_width * BLOCK, head_count, head_width
        )
        scores = (
            jnp.einsum(
                "gqhd,gkhd->ghqk", query_group, key_group, preferred_element_type=jnp.float32
            )
            * score_scale
        )
        row_max = jnp.max(scores, axis=-1, keepdims=True)
        exp_scores = jnp.exp(scores - row_max)
        totals = jnp.sum(exp_scores, axis=-1)
        weights_bf = exp_scores.astype(jnp.bfloat16)
        summed = jnp.einsum(
            "ghqk,gkhd->gqhd", weights_bf, value_group, preferred_element_type=jnp.float32
        )
        return (summed / jnp.transpose(totals, (0, 2, 1))[..., None]).astype(jnp.bfloat16)

    attended = lax.map(attend_group, jnp.arange(block_count // group_size, dtype=jnp.int32))
    return attended.reshape(total_rows, head_count, head_width)


def attend_grouped(stacked, block_lists):
    query_rows, key_rows, value_rows = stacked
    total_rows = query_rows.shape[0]
    head_count = query_rows.shape[2]
    head_width = query_rows.shape[3]
    flat = tuple(
        (
            piece.reshape(total_rows, head_count, head_width)
            for piece in (query_rows, key_rows, value_rows)
        )
    )
    result = attend_heads(flat, block_lists)
    return result.reshape(total_rows, 1, head_count, head_width)


def temporal_mix(
    normed, step_block, decay_rates, skip_gains, state_in_weight, state_out_weight, post_gain
):
    frame_count, token_count, channel_count = normed.shape
    head_count = step_block.shape[2]
    head_width = channel_count // head_count
    flat_rows = normed.reshape(frame_count * token_count, channel_count)
    b_in = jnp.dot(flat_rows, state_in_weight, preferred_element_type=jnp.float32).reshape(
        frame_count, token_count, -1
    )
    c_out = jnp.dot(flat_rows, state_out_weight, preferred_element_type=jnp.float32).reshape(
        frame_count, token_count, -1
    )
    gram_matrix = jnp.einsum("tkn,skn->kts", c_out, b_in, precision=lax.Precision.HIGHEST)
    log_decay = -step_block * decay_rates
    frame_index = jnp.arange(frame_count, dtype=jnp.int32)
    between = (
        (frame_index[None, :, None] < frame_index[None, None, :])
        & (frame_index[None, None, :] <= frame_index[:, None, None])
    ).astype(jnp.float32)
    seg_sum = jnp.einsum("tsr,rkh->ktsh", between, log_decay, precision=lax.Precision.HIGHEST)
    causal = frame_index[None, :] <= frame_index[:, None]
    decay_matrix = jnp.where(causal[None, :, :, None], jnp.exp(seg_sum), jnp.zeros_like(seg_sum))
    weight_matrix = (
        gram_matrix[..., None] * decay_matrix * jnp.transpose(step_block, (1, 0, 2))[:, None, :, :]
    )
    x_values = normed.astype(jnp.float32).reshape(frame_count, token_count, head_count, head_width)
    y_mixed = (
        jnp.einsum("ktsh,skhp->tkhp", weight_matrix, x_values, precision=lax.Precision.HIGHEST)
        + skip_gains[:, None] * x_values
    )
    y_flat = y_mixed.reshape(frame_count, token_count, channel_count)
    return rms_scale(y_flat, post_gain).astype(jnp.bfloat16)


def body(
    queries,
    key_vectors,
    value_vectors,
    block_lists,
    step_sizes,
    decay_rates,
    skip_gains,
    pre_gain,
    state_in_weight,
    state_out_weight,
    post_gain,
):
    token_count = queries.shape[1]
    channel_count = queries.shape[2]
    query_rows = queries.reshape(token_count, SHARED_HEADS, HEAD_DIM)
    key_rows = key_vectors.reshape(token_count, SHARED_HEADS, HEAD_DIM)
    value_rows = value_vectors.reshape(token_count, SHARED_HEADS, HEAD_DIM)
    by_token = None
    attended = None
    space_count = lax.axis_size("space")
    local_heads = SHARED_HEADS // space_count
    query_split = query_rows.reshape(token_count, space_count, local_heads, HEAD_DIM)
    key_split = key_rows.reshape(token_count, space_count, local_heads, HEAD_DIM)
    value_split = value_rows.reshape(token_count, space_count, local_heads, HEAD_DIM)
    received = attend_grouped(
        (
            lax.all_to_all(query_split, "space", split_axis=1, concat_axis=0, tiled=True),
            lax.all_to_all(key_split, "space", split_axis=1, concat_axis=0, tiled=True),
            lax.all_to_all(value_split, "space", split_axis=1, concat_axis=0, tiled=True),
        ),
        block_lists=block_lists,
    )
    gathered = received.reshape(received.shape[0], local_heads, HEAD_DIM)
    attended = lax.all_to_all(gathered, "space", split_axis=0, concat_axis=1, tiled=True)
    normed = rms_scale(
        attended.reshape(1, token_count, channel_count).astype(jnp.float32), pre_gain
    ).astype(jnp.bfloat16)
    by_token = lax.all_to_all(normed, "tm", split_axis=1, concat_axis=0, tiled=True)
    mixed_tokens = temporal_mix(
        by_token, step_sizes, decay_rates, skip_gains, state_in_weight, state_out_weight, post_gain
    )
    return lax.all_to_all(mixed_tokens, "tm", split_axis=0, concat_axis=1, tiled=True)


def solution(mesh):
    placed = (
        P("tm", "space", None),
        P("tm", "space", None),
        P("tm", "space", None),
        P(),
        P(None, ("space", "tm"), None),
        P(),
        P(),
        P(),
        P(),
        P(),
        P(),
    )
    return jax.shard_map(
        body, mesh=mesh, in_specs=placed, out_specs=P("tm", "space", None), check_vma=False
    )
```

profile of v0, /device:TPU:0, one launch (start us, length us, event | category | flops | bytes accessed | tf_op | source)
XLA Modules:
  0.0 110.1 jit_solution(432417027500597041)
XLA Ops:
  0.0 0.0 copy-start
  0.0 1.4 %copy.111 = bf16[1,128,2048]{1,2,0:T(8,128)(2,1)S(1)} copy(bf16[1,128,2048]{2,1,0:T(8,128)(2,1)} %param.14) | data formatting | bytes 1048576 | tf_op args[1]
  1.4 1.1 copy.112
  2.5 4.2 %all-to-all-start.1 = ((bf16[128,4,4,128]{3,2,0,1:T(4,128)(2,1)}), bf16[128,4,4,128]{3,2,0,1:T(4,128)(2,1)S(1)}, u32[]{:S(2)}, u32[]{:S(2)}) async-start(bf16[128,4,4,128]{3,2,0,1:T(4,128)(2,1)} %copy.112), calls=%async_computation.1 | async-start | bytes 1048576 | tf_op jit(solution)/shard_map/all_to_all | solution.py:134
  6.7 0.0 copy-done.2
  6.7 0.3 copy.108
  7.0 1.1 copy.109
  8.1 7.5 %all-to-all-done.1 = bf16[128,4,4,128]{3,2,0,1:T(4,128)(2,1)S(1)} async-done(((bf16[128,4,4,128]{3,2,0,1:T(4,128)(2,1)}), bf16[128,4,4,128]{3,2,0,1:T(4,128)(2,1)S(1)}, u32[]{:S(2)}, u32[]{:S(2)}) %all-to-all-start.1) | async-done | bytes 524320 | tf_op jit(solution)/shard_map/all_to_all | solution.py:134
  15.5 3.5 %all-to-all-start = ((bf16[128,4,4,128]{3,2,0,1:T(4,128)(2,1)}), bf16[128,4,4,128]{3,2,0,1:T(4,128)(2,1)S(1)}, u32[]{:S(2)}, u32[]{:S(2)}) async-start(bf16[128,4,4,128]{3,2,0,1:T(4,128)(2,1)} %copy.109), calls=%async_computation | async-start | bytes 1048576 | tf_op jit(solution)/shard_map/all_to_all | solution.py:135
  19.0 0.0 copy-done.8
  19.0 0.1 reshape.214
  19.1 0.0 copy-done.3
  19.1 0.3 copy.114
  19.4 1.0 copy.115
  20.4 1.9 %gather_fusion.1 = bf16[12,128,4,128]{3,2,1,0:T(4,128)(2,1)S(1)} fusion(bf16[4,128,4,128]{3,2,1,0:T(4,128)(2,1)S(1)} %bitcast.92, s32[1024]{0:T(1024)S(1)} %pad_clamp_fusion), kind=kCustom, calls=%fused_computation.1.clone | custom fusion | bytes 3145776 | tf_op jit(solution)/shard_map/while/body/eval_jaxpr/jit(_take)/gather | solution.py:31
  22.4 5.5 %all-to-all-done = bf16[128,4,4,128]{3,2,0,1:T(4,128)(2,1)S(1)} async-done(((bf16[128,4,4,128]{3,2,0,1:T(4,128)(2,1)}), bf16[128,4,4,128]{3,2,0,1:T(4,128)(2,1)S(1)}, u32[]{:S(2)}, u32[]{:S(2)}) %all-to-all-start) | async-done | bytes 524320 | tf_op jit(solution)/shard_map/all_to_all | solution.py:135
  27.8 3.5 %all-to-all-start.2 = ((bf16[128,4,4,128]{3,0,2,1:T(8,128)(2,1)}), bf16[128,4,4,128]{3,0,2,1:T(8,128)(2,1)S(1)}, u32[]{:S(2)}, u32[]{:S(2)}) async-start(bf16[128,4,4,128]{3,0,2,1:T(8,128)(2,1)} %copy.115), calls=%async_computation.2 | async-start | bytes 1048576 | tf_op jit(solution)/shard_map/all_to_all | solution.py:133
  31.3 3.2 %gather_fusion = bf16[12,128,4,128]{3,2,1,0:T(4,128)(2,1)} fusion(bf16[4,128,4,128]{3,2,1,0:T(4,128)(2,1)S(1)} %bitcast.93, s32[1024]{0:T(1024)S(1)} %pad_clamp_fusion), kind=kCustom, calls=%fused_computation.clone | custom fusion | bytes 3145776 | tf_op jit(solution)/shard_map/while/body/eval_jaxpr/jit(_take)/gather | solution.py:34
  34.5 2.8 %broadcast_select_fusion = (bf16[4,3,128,4,128]{4,3,2,1,0:T(4,128)(2,1)S(1)}, bf16[4,3,128,4,128]{4,3,2,1,0:T(4,128)(2,1)S(1)}) fusion(bf16[4,3,128,4,128]{4,3,2,1,0:T(4,128)(2,1)S(1)} %bitcast.95, pred[4,3]{1,0:T(4,128)(4,1)S(1)} %compare_and_fusion, bf16[4,3,128,4,128]{4,3,2,1,0:T(4,128)(2,1)} %bitcast.96), kind=kLoop, calls=%fused_computation.10 | loop fusion | flops 1572864 | bytes 6291468 | tf_op jit(solution)/shard_map/while/body/eval_jaxpr/jit(_take)/select_n | solution.py:31
  37.3 1.6 %copy.110 = bf16[4,3,128,4,128]{4,2,1,3,0:T(8,128)(2,1)} copy(bf16[4,3,128,4,128]{4,3,2,1,0:T(4,128)(2,1)S(1)} %get-tuple-element.17) | data formatting | bytes 3145728 | tf_op jit(solution)/shard_map/while/body/eval_jaxpr/jit(_take)/select_n | solution.py:34
  38.9 0.4 copy.113
  39.3 0.9 all-to-all-done.2
  40.1 0.6 bitcast_reduce_fusion
  40.7 0.0 copy-start.1
  40.7 0.5 fusion.1
  41.3 0.9 copy-done.1
  42.1 1.0 fusion.18
  43.2 0.4 copy.118
  43.6 11.2 %all_to_all.75 = bf16[512,4,128]{2,1,0:T(4,128)(2,1)S(1)} all-to-all(bf16[512,4,128]{2,1,0:T(4,128)(2,1)S(1)} %copy.118), channel_id=1, replica_groups=mesh['tm'=8,'space'=4] {'space'}, dimensions={0} | all-to-all | bytes 1048576 | tf_op jit(solution)/shard_map/all_to_all | solution.py:140
  54.8 0.1 copy_convert_fusion
  54.9 0.0 copy-start.6
  54.9 0.3 copy.120
  55.2 0.2 multiply_reduce_fusion.1
  55.5 0.1 copy-done.6
  55.6 0.3 multiply_convert_fusion.1
  55.9 0.9 copy.121
  56.9 0.5 broadcast.154
  57.4 3.7 %reduce.7 = bf16[128,2048]{1,0:T(8,128)(2,1)S(1)} reduce(bf16[128,1,2048]{2,1,0:T(2,128)(2,1)S(1)} %bitcast.100, bf16[]{:T(256)} %broadcast.154), dimensions={1}, to_apply=%bitcast.81.reduce_sub_computation | reduce | bytes 1048578
  61.2 1.2 %reshape.227 = bf16[8,2,16384]{2,1,0:T(2,128)(2,1)} reshape(bf16[128,2048]{1,0:T(8,128)(2,1)S(1)} %reduce.7) | data formatting | bytes 1048576
  62.3 6.5 %all-to-all-start.4 = ((bf16[8,2,16384]{2,1,0:T(2,128)(2,1)}), bf16[8,2,16384]{2,1,0:T(2,128)(2,1)S(1)}, u32[]{:S(2)}, u32[]{:S(2)}) async-start(bf16[8,2,16384]{2,1,0:T(2,128)(2,1)} %reshape.227), calls=%async_computation.4 | async-start | bytes 1048576 | tf_op jit(solution)/shard_map/all_to_all | solution.py:144
  68.8 0.0 copy-done.5
  68.8 0.0 copy-done.9
  68.9 14.1 %all-to-all-done.4 = bf16[8,2,16384]{2,1,0:T(2,128)(2,1)S(1)} async-done(((bf16[8,2,16384]{2,1,0:T(2,128)(2,1)}), bf16[8,2,16384]{2,1,0:T(2,128)(2,1)S(1)}, u32[]{:S(2)}, u32[]{:S(2)}) %all-to-all-start.4) | async-done | bytes 524320 | tf_op jit(solution)/shard_map/all_to_all | solution.py:144
  82.9 0.5 reshape.228
  83.5 3.0 %bitcast_reduce_fusion.2 = bf16[128,2048]{1,0:T(8,128)(2,1)S(1)} fusion(bf16[128,1,2048]{2,1,0:T(2,128)(2,1)S(1)} %reshape.228), kind=kLoop, calls=%fused_computation.52 | loop fusion | bytes 1048576 | tf_op jit(solution)/shard_map/all_to_all | solution.py:144
  86.5 0.0 copy-start.4
  86.5 0.1 copy.136
  86.6 0.3 copy.135
  86.9 0.3 fusion.24
  87.2 0.2 copy-done.4
  87.4 0.3 fusion.26
  87.7 0.0 copy-start.10
  87.7 0.3 fusion.29
  88.0 0.4 fusion.14
  88.4 0.4 copy.127
  88.9 1.4 %multiply_reduce_fusion = (f32[8,16]{0,1:T(8,128)S(1)}, f32[8,16,16,128]{3,0,2,1:T(8,128)S(1)}) fusion(bf16[8,16,16,128]{3,2,1,0:T(8,128)(2,1)S(1)} %bitcast.108, f32[16]{0:T(128)S(1)} %copy-done.10, f32[16,8,8,16]{2,1,3,0:T(8,128)S(1)} %copy.127), kind=kOutput, calls=%fused_computation.23 | convolution fusion | flops 26476416 | bytes 1638976 | tf_op jit(solution)/shard_map/ktsh,skhp->tkhp/dot_general | solution.py:99
  90.3 0.2 copy.129
  90.5 0.0 copy-start.7
  90.5 0.2 reshape.191
  90.7 0.1 copy.130
  90.8 0.4 copy-done.7
  91.2 0.2 multiply_convert_fusion
  91.4 17.9 %all_to_all.76 = bf16[8,16,2048]{2,1,0:T(8,128)(2,1)S(1)} all-to-all(bf16[8,16,2048]{2,1,0:T(8,128)(2,1)S(1)} %multiply_convert_fusion), channel_id=1, replica_groups=mesh['tm'=8,'space'=4] {'tm'}, dimensions={0} | all-to-all | bytes 1048576 | tf_op jit(solution)/shard_map/all_to_all | solution.py:148
  109.3 0.8 copy.151
  (17 shorter events, 0.1 us)
Async XLA Ops:
  0.0 86.9 %copy-start = (bf16[2048,64]{0,1:T(8,128)(2,1)S(1)}, bf16[2048,64]{0,1:T(8,128)(2,1)}, u32[]{:S(2)}) copy-start(bf16[2048,64]{0,1:T(8,128)(2,1)} %param.21) | copy-start | bytes 786436
  0.0 6.7 %copy-start.2 = (bf16[1,128,2048]{2,1,0:T(8,128)(2,1)S(1)}, bf16[1,128,2048]{2,1,0:T(8,128)(2,1)}, u32[]{:S(2)}) copy-start(bf16[1,128,2048]{2,1,0:T(8,128)(2,1)} %param.15) | copy-start | bytes 1572868
  2.5 13.1 %all-to-all-start.1 = ((bf16[128,4,4,128]{3,2,0,1:T(4,128)(2,1)}), bf16[128,4,4,128]{3,2,0,1:T(4,128)(2,1)S(1)}, u32[]{:S(2)}, u32[]{:S(2)}) async-start(bf16[128,4,4,128]{3,2,0,1:T(4,128)(2,1)} %copy.112), calls=%async_computation.1 | async-start | bytes 1048576 | tf_op jit(solution)/shard_map/all_to_all | solution.py:134
  6.7 12.3 %copy-start.8 = (s32[4,3]{1,0:T(4,128)S(1)}, s32[4,3]{1,0:T(4,128)}, u32[]{:S(2)}) copy-start(s32[4,3]{1,0:T(4,128)} %param.16) | copy-start | bytes 148
  6.7 12.4 %copy-start.3 = (bf16[1,128,2048]{2,1,0:T(8,128)(2,1)S(1)}, bf16[1,128,2048]{2,1,0:T(8,128)(2,1)}, u32[]{:S(2)}) copy-start(bf16[1,128,2048]{2,1,0:T(8,128)(2,1)} %param.13) | copy-start | bytes 1572868
  15.5 12.3 %all-to-all-start = ((bf16[128,4,4,128]{3,2,0,1:T(4,128)(2,1)}), bf16[128,4,4,128]{3,2,0,1:T(4,128)(2,1)S(1)}, u32[]{:S(2)}, u32[]{:S(2)}) async-start(bf16[128,4,4,128]{3,2,0,1:T(4,128)(2,1)} %copy.109), calls=%async_computation | async-start | bytes 1048576 | tf_op jit(solution)/shard_map/all_to_all | solution.py:135
  27.8 12.3 %all-to-all-start.2 = ((bf16[128,4,4,128]{3,0,2,1:T(8,128)(2,1)}), bf16[128,4,4,128]{3,0,2,1:T(8,128)(2,1)S(1)}, u32[]{:S(2)}, u32[]{:S(2)}) async-start(bf16[128,4,4,128]{3,0,2,1:T(8,128)(2,1)} %copy.115), calls=%async_computation.2 | async-start | bytes 1048576 | tf_op jit(solution)/shard_map/all_to_all | solution.py:133
  40.7 1.4 %copy-start.1 = (bf16[4,3,128,4,128]{4,2,1,3,0:T(8,128)(2,1)S(1)}, bf16[4,3,128,4,128]{4,2,1,3,0:T(8,128)(2,1)}, u32[]{:S(2)}) copy-start(bf16[4,3,128,4,128]{4,2,1,3,0:T(8,128)(2,1)} %copy.110) | copy-start | bytes 4718596
  54.9 0.7 copy-start.6
  57.4 11.4 %copy-start.5 = (f32[8,16,16]{2,1,0:T(8,128)S(1)}, f32[8,16,16]{2,1,0:T(8,128)}, u32[]{:S(2)}) copy-start(f32[8,16,16]{2,1,0:T(8,128)} %param.17) | copy-start | bytes 24580
  57.4 11.4 %copy-start.9 = (f32[16]{0:T(128)S(1)}, f32[16]{0:T(128)}, u32[]{:S(2)}) copy-start(f32[16]{0:T(128)} %param.18) | copy-start | bytes 196
  62.3 20.6 %all-to-all-start.4 = ((bf16[8,2,16384]{2,1,0:T(2,128)(2,1)}), bf16[8,2,16384]{2,1,0:T(2,128)(2,1)S(1)}, u32[]{:S(2)}, u32[]{:S(2)}) async-start(bf16[8,2,16384]{2,1,0:T(2,128)(2,1)} %reshape.227), calls=%async_computation.4 | async-start | bytes 1048576 | tf_op jit(solution)/shard_map/all_to_all | solution.py:144
  86.5 1.0 copy-start.4
  87.7 1.1 %copy-start.10 = (f32[16]{0:T(128)S(1)}, f32[16]{0:T(128)}, u32[]{:S(2)}) copy-start(f32[16]{0:T(128)} %param.19) | copy-start | bytes 196
  90.5 0.7 copy-start.7
where the time goes:
time: 111 us; the launch traced here: 110 us
  blocking collectives  29.1 us (26%)
  waiting for transfers between devices  27.9 us (25%)
  local copies, waits for them, and re-layouts  22.8 us (21%)
  starting transfers between devices  17.6 us (16%)
  other arithmetic  7.92 us (7%)
  matrix products  4.28 us (4%)
    all_to_all x1, blocking collectives, body(): lax.all_to_all(mixed_tokens, 'tm', split_axis=0, concat_axis=1, tiled=True)  17.9 us
    all_to_all x1, waiting for transfers between devices, body(): lax.all_to_all(normed, 'tm', split_axis=1, concat_axis=0, tiled=True)  14.1 us
    all_to_all x1, blocking collectives, body(): lax.all_to_all(gathered, 'space', split_axis=0, concat_axis=1, tiled=True)  11.2 us
    all_to_all x1, waiting for transfers between devices, body(): lax.all_to_all(key_split, 'space', split_axis=1, concat_axis=0, tiled=True)  7.49 us
    unnamed x31, local copies, waits for them, and re-layouts  7.03 us
    all_to_all x1, starting transfers between devices, body(): lax.all_to_all(normed, 'tm', split_axis=1, concat_axis=0, tiled=True)  6.46 us
    all_to_all x1, waiting for transfers between devices, body(): lax.all_to_all(value_split, 'space', split_axis=1, concat_axis=0, tiled=T...  5.49 us
    all_to_all x1, starting transfers between devices, body(): lax.all_to_all(key_split, 'space', split_axis=1, concat_axis=0, tiled=True)  4.24 us
  transfers between devices with their start and end apart: 4, of which 4 were waited for; matrix products, arithmetic and copies ran while one was open for 11% of the time, Pallas kernels for 0%

commit v1 on v0

--- a/solution.py
+++ b/solution.py
@@ -7,6 +7,20 @@
 SHARED_HEADS = 16
 HEAD_DIM = 128
 BLOCK = 128
+
+
+def spread_cards(u, out_dim, array_in):
+    built = u.shape
+    main = u.reshape(*built[:out_dim], array_in, built[out_dim] // array_in, *built[out_dim + 1 :])
+    return jnp.moveaxis(main, out_dim, 0)
+
+
+def _store_column(local, d_out):
+    local = jnp.moveaxis(local, 0, d_out)
+    earlier = local.shape
+    return local.reshape(
+        *earlier[:d_out], earlier[d_out] * earlier[d_out + 1], *earlier[d_out + 2 :]
+    )
 
 
 def rms_scale(values, gain_row):
@@ -128,10 +142,22 @@
     query_split = query_rows.reshape(token_count, space_count, local_heads, HEAD_DIM)
     key_split = key_rows.reshape(token_count, space_count, local_heads, HEAD_DIM)
     value_split = value_rows.reshape(token_count, space_count, local_heads, HEAD_DIM)
+
+    def _prepare_tasks(z_in, axis_tag, xin, z):
+        side_arr, h_now = (lax.psum(1, axis_tag), lax.axis_index(axis_tag))
+        t_next = spread_cards(z_in, xin, side_arr)
+        crops = [t_next[h_now]]
+        for i0 in range(1, side_arr):
+            clean = t_next[h_now ^ i0]
+            crops.append(lax.ppermute(clean, axis_tag, [(k0, k0 ^ i0) for k0 in range(side_arr)]))
+        met_up = jnp.stack(crops, axis=0)
+        t_next = met_up[h_now ^ jnp.arange(side_arr)]
+        return _store_column(t_next, z)
+
     received = attend_grouped(
         (
             lax.all_to_all(query_split, "space", split_axis=1, concat_axis=0, tiled=True),
-            lax.all_to_all(key_split, "space", split_axis=1, concat_axis=0, tiled=True),
+            _prepare_tasks(key_split, "space", 1, 0),
             lax.all_to_all(value_split, "space", split_axis=1, concat_axis=0, tiled=True),
         ),
         block_lists=block_lists,

time: 111 us -> 102 us (0.919)
  waiting for transfers between devices: 27.9 us -> 21.4 us
  local copies, waits for them, and re-layouts: 22.8 us -> 21.6 us
    all_to_all x1 -> x0, waiting for transfers between devices: 7.49 us -> none  [body(): lax.all_to_all(key_split, 'space', split_axis=1, concat_axis=0, tiled=True)]
    all_to_all x1 -> x0, starting transfers between devices: 4.24 us -> none  [body(): lax.all_to_all(key_split, 'space', split_axis=1, concat_axis=0, tiled=True)]
    ppermute x0 -> x3, starting transfers between devices: none -> 3.28 us  [_prepare_tasks(): lax.ppermute(clean, axis_tag, [(k0, k0 ^ i0) for k0 in range(side_arr)])]
    select_n x1, other arithmetic: 2.84 us -> 0.21 us  [attend_group(): jnp.take(key_blocks, chosen, axis=0)]
    select_n x1 -> x2, other arithmetic: 0.01 us -> 2.17 us  [attend_group(): jnp.take(value_blocks, chosen, axis=0)]
    unnamed x31 -> x34, local copies, waits for them, and re-layouts: 7.03 us -> 5.85 us
  transfers between devices with their start and end apart: 4 -> 6, of which waited for: 4 -> 3; matrix products, arithmetic and copies ran while one was open for 11% -> 12% of each run, Pallas kernels for 0% -> 0%
where the time goes in v1:
time: 102 us; the launch traced here: 101 us
  blocking collectives  29.1 us (29%)
  local copies, waits for them, and re-layouts  21.6 us (21%)
  waiting for transfers between devices  21.4 us (21%)
  starting transfers between devices  16.5 us (16%)
  other arithmetic  7.54 us (7%)
  matrix products  4.28 us (4%)
    all_to_all x1, blocking collectives, body(): lax.all_to_all(mixed_tokens, 'tm', split_axis=0, concat_axis=1, tiled=True)  17.9 us
    all_to_all x1, waiting for transfers between devices, body(): lax.all_to_all(normed, 'tm', split_axis=1, concat_axis=0, tiled=True)  14.1 us
    all_to_all x1, blocking collectives, body(): lax.all_to_all(gathered, 'space', split_axis=0, concat_axis=1, tiled=True)  11.2 us
    all_to_all x1, starting transfers between devices, body(): lax.all_to_all(normed, 'tm', split_axis=1, concat_axis=0, tiled=True)  6.29 us
    unnamed x34, local copies, waits for them, and re-layouts  5.85 us
    all_to_all x1, waiting for transfers between devices, body(): lax.all_to_all(value_split, 'space', split_axis=1, concat_axis=0, tiled=T...  5.73 us
    unnamed x1, other arithmetic  3.74 us
    all_to_all x1, starting transfers between devices, body(): lax.all_to_all(value_split, 'space', split_axis=1, concat_axis=0, tiled=T...  3.47 us
  transfers between devices with their start and end apart: 6, of which 3 were waited for; matrix products, arithmetic and copies ran while one was open for 12% of the time, Pallas kernels for 0%

profile of v1, /device:TPU:0, one launch (start us, length us, event | category | flops | bytes accessed | tf_op | source)
XLA Modules:
  0.0 100.9 jit_solution(14381656075192199757)
XLA Ops:
  0.0 1.5 %reshape_reshape_reshape.9 = bf16[128,4,1,4,128]{4,3,1,0,2:T(4,128)(2,1)S(1)} reshape(bf16[1,128,2048]{2,1,0:T(8,128)(2,1)} %param.14) | data formatting | bytes 1048576 | tf_op jit(solution)/shard_map/reshape;reshape;reshape | solution.py:14
  1.5 0.2 constant_dynamic-slice_fusion.3
  1.7 3.0 %collective-permute-start.1 = (bf16[128,1,4,128]{3,0,2,1:T(8,128)(2,1)S(1)}, bf16[128,1,4,128]{3,0,2,1:T(8,128)(2,1)S(1)}, u32[]{:S(2)}, u32[]{:S(2)}) collective-permute-start(bf16[128,1,4,128]{3,0,2,1:T(8,128)(2,1)S(1)} %bitcast.123), channel_id=1, source_target_pairs={{0,2},{1,3},{2,0},{3,1},{4,6},{5,7},{6,4},{7,5},{8,10},{9,11},{10,... | collective-permute-start | bytes 393224 | tf_op jit(solution)/shard_map/ppermute | solution.py:152
  4.8 0.1 collective-permute-start.2
  4.9 0.0 copy-start.8
  4.9 0.0 copy-start.3
  4.9 0.2 collective-permute-start
  5.1 0.3 copy.135
  5.4 1.1 %copy.136 = bf16[128,4,4,128]{3,2,0,1:T(4,128)(2,1)} copy(bf16[128,4,4,128]{0,3,2,1:T(8,128)(2,1)S(1)} %bitcast.117) | data formatting | bytes 1048576 | tf_op jit(solution)/shard_map/reshape;reshape | solution.py:144
  6.4 3.5 %all-to-all-start = ((bf16[128,4,4,128]{3,2,0,1:T(4,128)(2,1)}), bf16[128,4,4,128]{3,2,0,1:T(4,128)(2,1)S(1)}, u32[]{:S(2)}, u32[]{:S(2)}) async-start(bf16[128,4,4,128]{3,2,0,1:T(4,128)(2,1)} %copy.136), calls=%async_computation | async-start | bytes 1048576 | tf_op jit(solution)/shard_map/all_to_all | solution.py:161
  10.0 0.1 reshape.247
  10.1 0.3 copy.143
  10.4 1.0 copy.144
  11.4 0.0 collective-permute-done.1
  11.4 0.1 maximum_bitcast_fusion
  11.5 0.6 gather_fusion
  12.2 0.8 gather_fusion.2
  13.0 5.7 %all-to-all-done = bf16[128,4,4,128]{3,2,0,1:T(4,128)(2,1)S(1)} async-done(((bf16[128,4,4,128]{3,2,0,1:T(4,128)(2,1)}), bf16[128,4,4,128]{3,2,0,1:T(4,128)(2,1)S(1)}, u32[]{:S(2)}, u32[]{:S(2)}) %all-to-all-start) | async-done | bytes 524320 | tf_op jit(solution)/shard_map/all_to_all | solution.py:161
  18.7 3.5 %all-to-all-start.1 = ((bf16[128,4,4,128]{3,0,2,1:T(8,128)(2,1)}), bf16[128,4,4,128]{3,0,2,1:T(8,128)(2,1)S(1)}, u32[]{:S(2)}, u32[]{:S(2)}) async-start(bf16[128,4,4,128]{3,0,2,1:T(8,128)(2,1)} %copy.144), calls=%async_computation.1 | async-start | bytes 1048576 | tf_op jit(solution)/shard_map/all_to_all | solution.py:159
  22.2 0.2 broadcast_select_fusion
  22.4 0.2 copy.142
  22.6 3.2 %gather_fusion.1 = bf16[12,128,4,128]{3,2,1,0:T(4,128)(2,1)} fusion(bf16[4,128,4,128]{3,2,1,0:T(4,128)(2,1)S(1)} %bitcast.105, s32[1024]{0:T(1024)S(1)} %pad_clamp_fusion.1), kind=kCustom, calls=%fused_computation.clone | custom fusion | bytes 3145776 | tf_op jit(solution)/shard_map/while/body/eval_jaxpr/jit(_take)/gather | solution.py:48
  25.8 2.2 %broadcast_select_fusion.1 = bf16[4,3,128,4,128]{4,3,2,1,0:T(4,128)(2,1)S(1)} fusion(bf16[4,3,128,4,128]{4,3,2,1,0:T(4,128)(2,1)} %bitcast.108, pred[4,3]{1,0:T(4,128)(4,1)S(1)} %compare_and_fusion), kind=kLoop, calls=%fused_computation.12 | loop fusion | flops 786432 | bytes 3145740 | tf_op jit(solution)/shard_map/while/body/eval_jaxpr/jit(_take)/select_n | solution.py:48
  27.9 1.5 %copy.137 = bf16[4,3,128,4,128]{4,2,1,3,0:T(8,128)(2,1)} copy(bf16[4,3,128,4,128]{4,3,2,1,0:T(4,128)(2,1)S(1)} %broadcast_select_fusion.1) | data formatting | bytes 3145728 | tf_op jit(solution)/shard_map/while/body/eval_jaxpr/jit(_take)/select_n | solution.py:48
  29.5 1.5 %all-to-all-done.1 = bf16[128,4,4,128]{3,0,2,1:T(8,128)(2,1)S(1)} async-done(((bf16[128,4,4,128]{3,0,2,1:T(8,128)(2,1)}), bf16[128,4,4,128]{3,0,2,1:T(8,128)(2,1)S(1)}, u32[]{:S(2)}, u32[]{:S(2)}) %all-to-all-start.1) | async-done | bytes 524320 | tf_op jit(solution)/shard_map/all_to_all | solution.py:159
  31.0 0.6 bitcast_reduce_fusion
  31.6 0.5 fusion.1
  32.2 0.9 copy-done.1
  33.0 1.0 fusion.18
  34.1 0.4 copy.147
  34.5 11.2 %all_to_all.60 = bf16[512,4,128]{2,1,0:T(4,128)(2,1)S(1)} all-to-all(bf16[512,4,128]{2,1,0:T(4,128)(2,1)S(1)} %copy.147), channel_id=1, replica_groups=mesh['tm'=8,'space'=4] {'space'}, dimensions={0} | all-to-all | bytes 1048576 | tf_op jit(solution)/shard_map/all_to_all | solution.py:166
  45.7 0.1 copy_convert_fusion
  45.8 0.0 copy-start.6
  45.8 0.3 copy.149
  46.1 0.2 multiply_reduce_fusion.1
  46.4 0.1 copy-done.6
  46.5 0.3 multiply_convert_fusion.1
  46.8 0.9 copy.150
  47.8 0.5 broadcast.189
  48.3 3.7 %reduce.7 = bf16[128,2048]{1,0:T(8,128)(2,1)S(1)} reduce(bf16[128,1,2048]{2,1,0:T(2,128)(2,1)S(1)} %bitcast.112, bf16[]{:T(256)} %broadcast.189), dimensions={1}, to_apply=%bitcast.90.reduce_sub_computation | reduce | bytes 1048578
  52.0 1.2 %reshape.260 = bf16[8,2,16384]{2,1,0:T(2,128)(2,1)} reshape(bf16[128,2048]{1,0:T(8,128)(2,1)S(1)} %reduce.7) | data formatting | bytes 1048576
  53.2 6.3 %all-to-all-start.3 = ((bf16[8,2,16384]{2,1,0:T(2,128)(2,1)}), bf16[8,2,16384]{2,1,0:T(2,128)(2,1)S(1)}, u32[]{:S(2)}, u32[]{:S(2)}) async-start(bf16[8,2,16384]{2,1,0:T(2,128)(2,1)} %reshape.260), calls=%async_computation.3 | async-start | bytes 1048576 | tf_op jit(solution)/shard_map/all_to_all | solution.py:170
  59.6 14.1 %all-to-all-done.3 = bf16[8,2,16384]{2,1,0:T(2,128)(2,1)S(1)} async-done(((bf16[8,2,16384]{2,1,0:T(2,128)(2,1)}), bf16[8,2,16384]{2,1,0:T(2,128)(2,1)S(1)}, u32[]{:S(2)}, u32[]{:S(2)}) %all-to-all-start.3) | async-done | bytes 524320 | tf_op jit(solution)/shard_map/all_to_all | solution.py:170
  73.7 0.5 reshape.261
  74.2 3.0 %bitcast_reduce_fusion.2 = bf16[128,2048]{1,0:T(8,128)(2,1)S(1)} fusion(bf16[128,1,2048]{2,1,0:T(2,128)(2,1)S(1)} %reshape.261), kind=kLoop, calls=%fused_computation.65 | loop fusion | bytes 1048576 | tf_op jit(solution)/shard_map/all_to_all | solution.py:170
  77.2 0.0 copy-start.4
  77.2 0.3 copy.164
  77.5 0.3 fusion.24
  77.8 0.3 copy-done.4
  78.2 0.3 fusion.26
  78.5 0.3 fusion.29
  78.7 0.0 copy-start.10
  78.7 0.4 fusion.14
  79.2 0.4 copy.156
  79.6 0.1 copy.169
  79.7 1.4 %multiply_reduce_fusion = (f32[8,16]{0,1:T(8,128)S(1)}, f32[8,16,16,128]{3,0,2,1:T(8,128)S(1)}) fusion(bf16[8,16,16,128]{3,2,1,0:T(8,128)(2,1)S(1)} %bitcast.119, f32[16]{0:T(128)S(1)} %copy-done.10, f32[16,8,8,16]{2,1,3,0:T(8,128)S(1)} %copy.156), kind=kOutput, calls=%fused_computation.24 | convolution fusion | flops 26476416 | bytes 1638976 | tf_op jit(solution)/shard_map/ktsh,skhp->tkhp/dot_general | solution.py:113
  81.2 0.2 copy.158
  81.4 0.0 copy-start.7
  81.4 0.2 reshape.213
  81.5 0.1 copy.159
  81.6 0.4 copy-done.7
  82.1 0.2 multiply_convert_fusion
  82.2 17.9 %all_to_all.61 = bf16[8,16,2048]{2,1,0:T(8,128)(2,1)S(1)} all-to-all(bf16[8,16,2048]{2,1,0:T(8,128)(2,1)S(1)} %multiply_convert_fusion), channel_id=1, replica_groups=mesh['tm'=8,'space'=4] {'tm'}, dimensions={0} | all-to-all | bytes 1048576 | tf_op jit(solution)/shard_map/all_to_all | solution.py:174
  100.1 0.8 copy.192
  (30 shorter events, 0.3 us)
Async XLA Ops:
  0.0 77.5 %copy-start = (bf16[2048,64]{0,1:T(8,128)(2,1)S(1)}, bf16[2048,64]{0,1:T(8,128)(2,1)}, u32[]{:S(2)}) copy-start(bf16[2048,64]{0,1:T(8,128)(2,1)} %param.21) | copy-start | bytes 786436
  0.0 5.1 %copy-start.2 = (bf16[1,128,2048]{2,1,0:T(8,128)(2,1)S(1)}, bf16[1,128,2048]{2,1,0:T(8,128)(2,1)}, u32[]{:S(2)}) copy-start(bf16[1,128,2048]{2,1,0:T(8,128)(2,1)} %param.15) | copy-start | bytes 1572868
  1.7 9.7 %collective-permute-start.1 = (bf16[128,1,4,128]{3,0,2,1:T(8,128)(2,1)S(1)}, bf16[128,1,4,128]{3,0,2,1:T(8,128)(2,1)S(1)}, u32[]{:S(2)}, u32[]{:S(2)}) collective-permute-start(bf16[128,1,4,128]{3,0,2,1:T(8,128)(2,1)S(1)} %bitcast.123), channel_id=1, source_target_pairs={{0,2},{1,3},{2,0},{3,1},{4,6},{5,7},{6,4},{7,5},{8,10},{9,11},{10,... | collective-permute-start | bytes 393224 | tf_op jit(solution)/shard_map/ppermute | solution.py:152
  4.8 6.6 %collective-permute-start.2 = (bf16[128,1,4,128]{3,0,2,1:T(8,128)(2,1)S(1)}, bf16[128,1,4,128]{3,0,2,1:T(8,128)(2,1)S(1)}, u32[]{:S(2)}, u32[]{:S(2)}) collective-permute-start(bf16[128,1,4,128]{3,0,2,1:T(8,128)(2,1)S(1)} %bitcast.124), channel_id=1, source_target_pairs={{0,3},{1,2},{2,1},{3,0},{4,7},{5,6},{6,5},{7,4},{8,11},{9,10},{10,... | collective-permute-start | bytes 393224 | tf_op jit(solution)/shard_map/ppermute | solution.py:152
  4.9 5.0 %copy-start.8 = (s32[4,3]{1,0:T(4,128)S(1)}, s32[4,3]{1,0:T(4,128)}, u32[]{:S(2)}) copy-start(s32[4,3]{1,0:T(4,128)} %param.16) | copy-start | bytes 148
  4.9 5.2 %copy-start.3 = (bf16[1,128,2048]{2,1,0:T(8,128)(2,1)S(1)}, bf16[1,128,2048]{2,1,0:T(8,128)(2,1)}, u32[]{:S(2)}) copy-start(bf16[1,128,2048]{2,1,0:T(8,128)(2,1)} %param.13) | copy-start | bytes 1572868
  4.9 6.5 %collective-permute-start = (bf16[128,1,4,128]{3,0,2,1:T(8,128)(2,1)S(1)}, bf16[128,1,4,128]{3,0,2,1:T(8,128)(2,1)S(1)}, u32[]{:S(2)}, u32[]{:S(2)}) collective-permute-start(bf16[128,1,4,128]{3,0,2,1:T(8,128)(2,1)S(1)} %bitcast.125), channel_id=1, source_target_pairs={{0,1},{1,0},{2,3},{3,2},{4,5},{5,4},{6,7},{7,6},{8,9},{9,8},{10,11... | collective-permute-start | bytes 393224 | tf_op jit(solution)/shard_map/ppermute | solution.py:152
  6.4 12.3 %all-to-all-start = ((bf16[128,4,4,128]{3,2,0,1:T(4,128)(2,1)}), bf16[128,4,4,128]{3,2,0,1:T(4,128)(2,1)S(1)}, u32[]{:S(2)}, u32[]{:S(2)}) async-start(bf16[128,4,4,128]{3,2,0,1:T(4,128)(2,1)} %copy.136), calls=%async_computation | async-start | bytes 1048576 | tf_op jit(solution)/shard_map/all_to_all | solution.py:161
  18.7 12.3 %all-to-all-start.1 = ((bf16[128,4,4,128]{3,0,2,1:T(8,128)(2,1)}), bf16[128,4,4,128]{3,0,2,1:T(8,128)(2,1)S(1)}, u32[]{:S(2)}, u32[]{:S(2)}) async-start(bf16[128,4,4,128]{3,0,2,1:T(8,128)(2,1)} %copy.144), calls=%async_computation.1 | async-start | bytes 1048576 | tf_op jit(solution)/shard_map/all_to_all | solution.py:159
  31.6 1.4 %copy-start.1 = (bf16[4,3,128,4,128]{4,2,1,3,0:T(8,128)(2,1)S(1)}, bf16[4,3,128,4,128]{4,2,1,3,0:T(8,128)(2,1)}, u32[]{:S(2)}) copy-start(bf16[4,3,128,4,128]{4,2,1,3,0:T(8,128)(2,1)} %copy.137) | copy-start | bytes 4718596
  45.8 0.7 copy-start.6
  48.3 11.2 %copy-start.5 = (f32[8,16,16]{2,1,0:T(8,128)S(1)}, f32[8,16,16]{2,1,0:T(8,128)}, u32[]{:S(2)}) copy-start(f32[8,16,16]{2,1,0:T(8,128)} %param.17) | copy-start | bytes 24580
  48.3 11.3 %copy-start.9 = (f32[16]{0:T(128)S(1)}, f32[16]{0:T(128)}, u32[]{:S(2)}) copy-start(f32[16]{0:T(128)} %param.18) | copy-start | bytes 196
  53.2 20.5 %all-to-all-start.3 = ((bf16[8,2,16384]{2,1,0:T(2,128)(2,1)}), bf16[8,2,16384]{2,1,0:T(2,128)(2,1)S(1)}, u32[]{:S(2)}, u32[]{:S(2)}) async-start(bf16[8,2,16384]{2,1,0:T(2,128)(2,1)} %reshape.260), calls=%async_computation.3 | async-start | bytes 1048576 | tf_op jit(solution)/shard_map/all_to_all | solution.py:170
  77.2 1.0 copy-start.4
  78.7 1.0 copy-start.10
  81.4 0.7 copy-start.7
